TPU v7x, 32 devices: a whole 2x2x4 slice. The times are simulated.
32 devices in a mesh: dp: 4 (over x, core), group: 4 (over z), tensor: 2 (over y).
Axes of the slice: x: 2, y: 2, z: 4, core: 2. Of those that a mesh axis runs over, the one named last changes fastest.
Arguments:
- residual_in: bfloat16 [32, 1024, 767], P(('dp', 'group'), 'tensor'), may hold values from -6 to 6
- piece_ids: int32 [32, 1024], P(('dp', 'group')), may hold values from -1 to 3, as said below
- norm_gains: bfloat16 [2, 768], replicated, may hold values from 0.25 to 1.75
- qkv_weight: bfloat16 [3, 768, 768], P(None, None, 'tensor'), may hold values from -0.21875 to 0.21875
- qv_bias: bfloat16 [2, 768], P(None, 'tensor'), may hold values from -3 to 3
- out_weight: bfloat16 [768, 767], P('tensor'), may hold values from -0.875 to 0.875
- fc_weight: bfloat16 [768, 3072], P(None, 'tensor'), may hold values from -0.21875 to 0.21875
- fc_bias: bfloat16 [3072], P('tensor'), may hold values from -3 to 3
- proj_weight: bfloat16 [3072, 767], P('tensor'), may hold values from -0.109375 to 0.109375
- out_biases: bfloat16 [2, 767], replicated, may hold values from -2 to 2
- cotangent: bfloat16 [32, 1024, 767], P(('dp', 'group'), 'tensor'), may hold values from -6 to 6
Outputs:
- block_out: bfloat16 [32, 1024, 767], P(('dp', 'group'), 'tensor')
- grad_input: bfloat16 [32, 1024, 767], P(('dp', 'group'), 'tensor')
- grad_gains: float32 [2, 768], replicated
- grad_qkv: float32 [3, 768, 768], P(None, 'dp', 'tensor')
- grad_qv_bias: float32 [2, 768], P(None, ('tensor', 'dp'))
- grad_out_weight: float32 [768, 767], P(('tensor', 'dp'))
- grad_fc_weight: float32 [768, 3072], P('dp', 'tensor')
- grad_fc_bias: float32 [3072], P(('tensor', 'dp'))
- grad_proj_weight: float32 [3072, 767], P(('tensor', 'dp'))
- grad_out_biases: float32 [2, 767], replicated
Inputs may be any that keep to these rules, and one draw needn't show every extreme that they name: `piece_ids`: each aligned block of 256 positions of a sequence carries one id: -1 (text) or the block's own number (a picture piece). The first block of every sequence is text and the last one a picture piece.
All inputs are finite; a program needn't handle non-finite values.
Results may differ from a plain program's by a relative error of at most 0.02.
Values may be sent and summed in bfloat16 or wider, within the bound.
No kernel may reach another device: no remote copies, remote signals or barrier semaphores. Data moves between devices by JAX's collectives and lax.ppermute only.
A program may use at most 192 MiB of HBM per device.

v0:
```python
import jax
import jax.numpy as jnp
from jax import lax
from jax.sharding import PartitionSpec as P

D = 768
HD = 64
EPSILON = 1e-05
MASKED = -1e30


def decompress(compact):
    return jnp.concatenate([compact, -jnp.sum(compact, axis=-1, keepdims=True)], axis=-1)


def crms_gain(compact, gain):
    full_rows = decompress(compact)
    factor = lax.rsqrt(jnp.mean(full_rows * full_rows, axis=-1, keepdims=True) + EPSILON)
    return full_rows * factor * gain


def gelu_tanh(values):
    return jax.nn.gelu(values, approximate=True)


def visible_mask(labels, row_start, row_count):
    query_pos = row_start + jnp.arange(row_count)
    key_pos = jnp.arange(labels.shape[0])
    row_labels = labels[row_start : row_start + row_count]
    causal = key_pos[None, :] <= query_pos[:, None]
    inside = (row_labels[:, None] == labels[None, :]) & (row_labels[:, None] >= 0)
    return causal | inside


def block_scores(row_query, key_rows, labels, row_start, row_block):
    scores = jnp.einsum(
        "qhd,khd->hqk", row_query, key_rows, preferred_element_type=jnp.float32
    ) * HD ** (-0.5)
    return jnp.where(visible_mask(labels, row_start, row_block)[None], scores, MASKED)


def attend_forward(inputs):
    queries, key_rows, value_rows, labels = inputs
    length = key_rows.shape[0]
    row_block = min(512, length)
    outputs = []
    log_parts = []
    for row_start in range(0, length, row_block):
        scores = block_scores(
            queries[row_start : row_start + row_block], key_rows, labels, row_start, row_block
        )
        highest = jnp.max(scores, axis=-1, keepdims=True)
        weights = jnp.exp(scores - highest)
        weight_sum = jnp.sum(weights, axis=-1, keepdims=True)
        prob_low = (weights / weight_sum).astype(jnp.bfloat16)
        outputs.append(
            jnp.einsum(
                "hqk,khd->qhd", prob_low, value_rows, preferred_element_type=jnp.float32
            ).astype(jnp.bfloat16)
        )
        log_parts.append((highest + jnp.log(weight_sum))[..., 0])
    return (jnp.concatenate(outputs, 0), jnp.concatenate(log_parts, 1))


def attend_backward(inputs):
    queries, key_rows, value_rows, labels, upstream, log_sums = inputs
    length = key_rows.shape[0]
    row_block = min(512, length)
    score_scale = HD ** (-0.5)
    grad_keys = jnp.zeros(key_rows.shape, jnp.float32)
    grad_values = jnp.zeros(value_rows.shape, jnp.float32)
    query_grads = []
    for row_start in range(0, length, row_block):
        row_query = queries[row_start : row_start + row_block]
        row_up = upstream[row_start : row_start + row_block]
        scores = block_scores(row_query, key_rows, labels, row_start, row_block)
        probs = jnp.exp(scores - log_sums[:, row_start : row_start + row_block, None])
        along = jnp.einsum("qhd,khd->hqk", row_up, value_rows, preferred_element_type=jnp.float32)
        inner = jnp.sum(along * probs, axis=-1, keepdims=True)
        score_grad = (probs * (along - inner)).astype(jnp.bfloat16)
        query_grads.append(
            jnp.einsum("hqk,khd->qhd", score_grad, key_rows, preferred_element_type=jnp.float32)
            * score_scale
        )
        grad_keys = (
            grad_keys
            + jnp.einsum("hqk,qhd->khd", score_grad, row_query, preferred_element_type=jnp.float32)
            * score_scale
        )
        grad_values = grad_values + jnp.einsum(
            "hqk,qhd->khd", probs.astype(jnp.bfloat16), row_up, preferred_element_type=jnp.float32
        )
    return (jnp.concatenate(query_grads, 0), grad_keys, grad_values)


def on_device(
    residual_in,
    piece_ids,
    norm_gains,
    qkv_weight,
    qv_bias,
    out_weight,
    fc_weight,
    fc_bias,
    proj_weight,
    out_biases,
    cotangent,
):
    residual_rows, upstream_rows, labels_all = (residual_in, cotangent, piece_ids)
    qkv_w, qv_b, out_w, fc_w, fc_b, proj_w = (
        qkv_weight,
        qv_bias,
        out_weight,
        fc_weight,
        fc_bias,
        proj_weight,
    )
    seq_count, local_len, compact_width = residual_rows.shape
    local_rows = seq_count * local_len
    local_width = qkv_w.shape[2]
    head_count = local_width // HD
    gain_values = norm_gains.astype(jnp.float32)
    bias_values = qv_b.astype(jnp.float32)
    end_biases = out_biases.astype(jnp.float32)
    inputs_flat = residual_rows.reshape(local_rows, compact_width).astype(jnp.float32)
    normed_one, norm_one_back = jax.vjp(crms_gain, inputs_flat, gain_values[0])
    one_low = normed_one.astype(jnp.bfloat16).reshape(seq_count, local_len, D)
    full_one = lax.all_gather(one_low, "tensor", axis=1, tiled=True)
    seq_len = full_one.shape[1]
    token_count = seq_count * seq_len
    flat_one = full_one.reshape(token_count, D)
    projected = jnp.einsum("td,cde->cte", flat_one, qkv_w, preferred_element_type=jnp.float32)
    queries = (
        (projected[0] + bias_values[0])
        .astype(jnp.bfloat16)
        .reshape(seq_count, seq_len, head_count, HD)
    )
    key_rows = projected[1].astype(jnp.bfloat16).reshape(seq_count, seq_len, head_count, HD)
    value_rows = (
        (projected[2] + bias_values[1])
        .astype(jnp.bfloat16)
        .reshape(seq_count, seq_len, head_count, HD)
    )
    attended, log_sums = lax.map(attend_forward, (queries, key_rows, value_rows, labels_all))
    attended_flat = attended.reshape(token_count, local_width)
    branch_part = jnp.dot(attended_flat, out_w, preferred_element_type=jnp.float32).reshape(
        seq_count, seq_len, compact_width
    )
    branch_sum = lax.psum_scatter(
        branch_part.astype(jnp.bfloat16), "tensor", scatter_dimension=1, tiled=True
    ).astype(jnp.float32)
    middle = inputs_flat + branch_sum.reshape(local_rows, compact_width) + end_biases[0]
    normed_two, norm_two_back = jax.vjp(crms_gain, middle, gain_values[1])
    two_low = normed_two.astype(jnp.bfloat16).reshape(seq_count, local_len, D)
    full_two = lax.all_gather(two_low, "tensor", axis=1, tiled=True).reshape(token_count, D)
    hidden_pre = jnp.dot(full_two, fc_w, preferred_element_type=jnp.float32) + fc_b.astype(
        jnp.float32
    )
    active_full, gelu_back = jax.vjp(gelu_tanh, hidden_pre)
    active = active_full.astype(jnp.bfloat16)
    mlp_part = jnp.dot(active, proj_w, preferred_element_type=jnp.float32).reshape(
        seq_count, seq_len, compact_width
    )
    mlp_sum = lax.psum_scatter(
        mlp_part.astype(jnp.bfloat16), "tensor", scatter_dimension=1, tiled=True
    ).astype(jnp.float32)
    block_out = (
        (middle + mlp_sum.reshape(local_rows, compact_width) + end_biases[1])
        .astype(jnp.bfloat16)
        .reshape(seq_count, local_len, compact_width)
    )
    upstream_full = lax.all_gather(upstream_rows, "tensor", axis=1, tiled=True).reshape(
        token_count, compact_width
    )
    upstream_flat = upstream_rows.reshape(local_rows, compact_width).astype(jnp.float32)
    grad_proj_weight = jnp.dot(active.T, upstream_full, preferred_element_type=jnp.float32)
    hidden_grad = gelu_back(jnp.dot(upstream_full, proj_w.T, preferred_element_type=jnp.float32))[
        0
    ].astype(jnp.bfloat16)
    grad_fc_weight = jnp.dot(full_two.T, hidden_grad, preferred_element_type=jnp.float32)
    grad_fc_bias = jnp.sum(hidden_grad.astype(jnp.float32), axis=0)
    two_part = jnp.dot(hidden_grad, fc_w.T, preferred_element_type=jnp.float32).reshape(
        seq_count, seq_len, D
    )
    two_grad = (
        lax.psum_scatter(two_part.astype(jnp.bfloat16), "tensor", scatter_dimension=1, tiled=True)
        .astype(jnp.float32)
        .reshape(local_rows, D)
    )
    middle_norm_grad, gain_two_grad = norm_two_back(two_grad)
    middle_grad = upstream_flat + middle_norm_grad
    branch_low = middle_grad.astype(jnp.bfloat16)
    branch_seq = branch_low.reshape(seq_count, local_len, compact_width)
    branch_full = lax.all_gather(branch_seq, "tensor", axis=1, tiled=True).reshape(
        token_count, compact_width
    )
    grad_out_weight = jnp.dot(attended_flat.T, branch_full, preferred_element_type=jnp.float32)
    attended_grad = (
        jnp.dot(branch_full, out_w.T, preferred_element_type=jnp.float32)
        .astype(jnp.bfloat16)
        .reshape(seq_count, seq_len, head_count, HD)
    )
    query_grad, key_grad, value_grad = lax.map(
        attend_backward, (queries, key_rows, value_rows, labels_all, attended_grad, log_sums)
    )
    stacked = (
        jnp.stack([query_grad, key_grad, value_grad])
        .astype(jnp.bfloat16)
        .reshape(3, token_count, local_width)
    )
    grad_qkv = jnp.einsum("td,cte->cde", flat_one, stacked, preferred_element_type=jnp.float32)
    grad_qv_bias = jnp.stack(
        [
            jnp.sum(stacked[0].astype(jnp.float32), axis=0),
            jnp.sum(stacked[2].astype(jnp.float32), axis=0),
        ]
    )
    one_part = jnp.einsum(
        "cte,cde->td", stacked, qkv_w, preferred_element_type=jnp.float32
    ).reshape(seq_count, seq_len, D)
    one_grad = (
        lax.psum_scatter(one_part.astype(jnp.bfloat16), "tensor", scatter_dimension=1, tiled=True)
        .astype(jnp.float32)
        .reshape(local_rows, D)
    )
    input_norm_grad, gain_one_grad = norm_one_back(one_grad)
    grad_input = (
        (middle_grad + input_norm_grad)
        .astype(jnp.bfloat16)
        .reshape(seq_count, local_len, compact_width)
    )
    gain_terms = jnp.stack([gain_one_grad, gain_two_grad])
    bias_terms = jnp.stack(
        [jnp.sum(branch_low.astype(jnp.float32), axis=0), jnp.sum(upstream_flat, axis=0)]
    )
    grad_gains, grad_out_biases = lax.psum((gain_terms, bias_terms), ("dp", "group", "tensor"))
    weight_grads = (
        grad_qkv,
        grad_qv_bias,
        grad_out_weight,
        grad_fc_weight,
        grad_fc_bias,
        grad_proj_weight,
    )
    shards = (
        lax.psum_scatter(
            weight_grads[0].astype(jnp.bfloat16), "dp", scatter_dimension=1, tiled=True
        ).astype(jnp.float32),
        lax.psum_scatter(
            weight_grads[1].astype(jnp.bfloat16), "dp", scatter_dimension=1, tiled=True
        ).astype(jnp.float32),
        lax.psum_scatter(
            weight_grads[2].astype(jnp.bfloat16), "dp", scatter_dimension=0, tiled=True
        ).astype(jnp.float32),
        lax.psum_scatter(
            weight_grads[3].astype(jnp.bfloat16), "dp", scatter_dimension=0, tiled=True
        ).astype(jnp.float32),
        lax.psum_scatter(
            weight_grads[4].astype(jnp.bfloat16), "dp", scatter_dimension=0, tiled=True
        ).astype(jnp.float32),
        lax.psum_scatter(
            weight_grads[5].astype(jnp.bfloat16), "dp", scatter_dimension=0, tiled=True
        ).astype(jnp.float32),
    )
    reduced = (
        lax.psum(shards[0].astype(jnp.bfloat16), "group").astype(jnp.float32),
        lax.psum(shards[1].astype(jnp.bfloat16), "group").astype(jnp.float32),
        lax.psum(shards[2].astype(jnp.bfloat16), "group").astype(jnp.float32),
        lax.psum(shards[3].astype(jnp.bfloat16), "group").astype(jnp.float32),
        lax.psum(shards[4].astype(jnp.bfloat16), "group").astype(jnp.float32),
        lax.psum(shards[5].astype(jnp.bfloat16), "group").astype(jnp.float32),
    )
    return (
        block_out,
        grad_input,
        grad_gains,
        reduced[0],
        reduced[1],
        reduced[2],
        reduced[3],
        reduced[4],
        reduced[5],
        grad_out_biases,
    )


def solution(mesh):
    in_specs = (
        P(("dp", "group"), "tensor", None),
        P(("dp", "group"), None),
        P(),
        P(None, None, "tensor"),
        P(None, "tensor"),
        P("tensor", None),
        P(None, "tensor"),
        P("tensor"),
        P("tensor", None),
        P(),
        P(("dp", "group"), "tensor", None),
    )
    out_specs = (
        P(("dp", "group"), "tensor", None),
        P(("dp", "group"), "tensor", None),
        P(),
        P(None, "dp", "tensor"),
        P(None, ("tensor", "dp")),
        P(("tensor", "dp"), None),
        P("dp", "tensor"),
        P(("tensor", "dp")),
        P(("tensor", "dp"), None),
        P(),
    )
    return jax.shard_map(
        on_device, mesh=mesh, in_specs=in_specs, out_specs=out_specs, check_vma=False
    )
```

profile of v0, /device:TPU:0, one launch (start us, length us, event | category | flops | bytes accessed | tf_op | source)
XLA Modules:
  0.0 1026.2 jit_solution(11230917446306738538)
XLA Ops:
  7.2 5.2 copy.65
  18.4 3.7 copy.67
  28.7 47.5 %all-gather.5.cloned.1.call-done = bf16[2,1024,768]{2,1,0:T(8,128)(2,1)} async-done(((bf16[2,512,768]{2,1,0:T(8,128)(2,1)}), bf16[2,1024,768]{2,1,0:T(8,128)(2,1)}) %all-gather.5.cloned.1.call-update) | async-done | bytes 3145744 | tf_op jit(solution)/shard_map/all_gather | solution.py:128
  76.2 6.8 convolution_bitcast_fusion
  90.9 5.6 squeeze.35
  103.8 3.9 convert_element_type.203
  114.3 5.6 squeeze.34
  124.6 54.4 %while.26 = (s32[]{:T(128)}, bf16[2,1024,6,64]{1,3,2,0:T(8,128)(2,1)}, f32[2,6,1024]{2,1,0:T(8,128)}, bf16[2,1024,6,64]{1,3,2,0:T(8,128)(2,1)}, s32[2,1024]{1,0:...) while((s32[]{:T(128)}, ...), condition=%wide.region_7.8_spmd, body=%wide.region_2.7_spmd.sunk | while | flops 1692272128 | bytes 111457016 | solution.py:144
  127.7 3.6 fusion.157
  131.3 3.6 fusion.158
  135.0 3.9 fusion.159
  146.0 3.9 fusion.162
  154.7 3.6 fusion.157
  162.0 3.9 fusion.159
  173.0 3.9 fusion.162
  179.0 4.8 convolution_convert_fusion.5
  185.3 42.1 %reduce-scatter.14.cloned.1.call-done = bf16[2,512,767]{2,1,0:T(8,128)(2,1)} async-done(((bf16[2,1024,767]{2,1,0:T(8,128)(2,1)}), bf16[2,512,767]{2,1,0:T(8,128)(2,1)}) %reduce-scatter.14.cloned.1.call-update) | async-done | bytes 1570832 | tf_op jit(solution)/shard_map/reduce_scatter | solution.py:149
  227.4 4.0 fusion.94
  234.9 3.9 add_add_fusion.2
  244.4 29.4 %all-gather.9.cloned.1.call-done = bf16[2,1024,767]{1,0,2:T(2,128)(2,1)} async-done(((bf16[2,512,767]{1,0,2:T(2,128)(2,1)}), bf16[2,1024,767]{1,0,2:T(2,128)(2,1)}) %all-gather.9.cloned.1.call-update) | async-done | bytes 3141648 | tf_op jit(solution)/shard_map/all_gather | solution.py:172
  273.9 4.3 pad.21
  280.9 39.4 %all-gather.7.cloned.1.call-done = bf16[2,1024,768]{2,1,0:T(8,128)(2,1)} async-done(((bf16[2,512,768]{2,1,0:T(8,128)(2,1)}), bf16[2,1024,768]{2,1,0:T(8,128)(2,1)}) %all-gather.7.cloned.1.call-update) | async-done | bytes 3145744 | tf_op jit(solution)/shard_map/all_gather | solution.py:155
  320.3 13.8 %multiply_convert_fusion.2 = (bf16[2048,1536]{1,0:T(8,128)(2,1)}, f32[2048,1536]{1,0:T(8,128)}) fusion(f32[1536]{0:T(1024)S(1)} %convert_element_type.208, bf16[2048,768]{1,0:T(8,128)(2,1)} %bitcast.353, bf16[768,1536]{1,0:T(8,128)(2,1)S(1)} %copy-done), kind=kOutput, calls=%fused_computation.125 | convolution fusion | flops 4863295488 | bytes 24385536 | tf_op jit(solution)/shard_map/dot_general | solution.py:156
  334.1 15.3 %fusion.97 = (bf16[1536]{0:T(1024)(128)(2,1)}, bf16[2048,1536]{1,0:T(8,128)(2,1)S(1)}) fusion(f32[2048,1536]{1,0:T(8,128)} %get-tuple-element.273, f32[1536]{0:T(1024)S(1)} %convert_element_type.208, bf16[2048,767]{0,1:T(8,128)(2,1)S(1)} %bitcast.318, bf16[1536,767]{1,0:T(8,128)(2,1)S(1)} %copy-done.63), kind=kOutput, calls=%fused_computation.195 | convolution fusion | flops 4894751232 | bytes 24381440 | tf_op jit(solution)/shard_map/dot_general | solution.py:177
  349.4 6.4 convolution_convert_fusion.2
  362.0 37.4 %reduce-scatter.18.cloned.1.call-done = bf16[2,512,768]{2,1,0:T(8,128)(2,1)} async-done(((bf16[2,1024,768]{2,1,0:T(8,128)(2,1)}), bf16[2,512,768]{2,1,0:T(8,128)(2,1)}) %reduce-scatter.18.cloned.1.call-update) | async-done | bytes 1572880 | tf_op jit(solution)/shard_map/reduce_scatter | solution.py:186
  412.4 44.9 %all-gather.11.cloned.1.call-done = bf16[2,1024,767]{1,0,2:T(2,128)(2,1)} async-done(((bf16[2,512,767]{1,0,2:T(2,128)(2,1)}), bf16[2,1024,767]{1,0,2:T(2,128)(2,1)}) %all-gather.11.cloned.1.call-update) | async-done | bytes 3141648 | tf_op jit(solution)/shard_map/all_gather | solution.py:194
  457.3 4.3 pad.22
  472.5 133.8 %while.27 = (s32[]{:T(128)}, bf16[2,1024,6,64]{1,3,2,0:T(8,128)(2,1)}, bf16[2,1024,6,64]{1,3,2,0:T(8,128)(2,1)}, bf16[2,1024,6,64]{1,3,2,0:T(8,128)(2,1)}, bf16[...) while((s32[]{:T(128)}, ...), condition=%wide.region_17.18_spmd, body=%wide.region_14.17_spmd.sunk | while | flops 4128632320 | bytes 286275584 | solution.py:203
  482.8 4.4 fusion.183
  487.3 5.5 bitcast_dynamic-update-slice_fusion.5
  492.8 8.4 multiply_reduce_fusion.10
  501.2 9.6 multiply_convert_fusion.7
  510.8 5.2 fusion.178
  516.0 8.1 multiply_reduce_fusion.11
  524.1 7.0 multiply_convert_fusion.8
  549.5 4.4 fusion.183
  553.9 5.5 bitcast_dynamic-update-slice_fusion.5
  559.4 8.4 multiply_reduce_fusion.10
  567.8 9.6 multiply_convert_fusion.7
  577.5 5.2 fusion.178
  582.7 8.1 multiply_reduce_fusion.11
  590.8 7.0 multiply_convert_fusion.8
  614.7 3.8 stack.48
  628.0 4.9 convert_bitcast_fusion.1
  632.9 4.0 copy.94
  638.5 9.4 convolution_convert_fusion
  648.0 9.4 convolution_convert_fusion.1
  663.5 9.0 convolution_convert_fusion.3
  678.5 25.3 %reduce-scatter.26.cloned.1.call-done = bf16[384,767]{1,0:T(8,128)(2,1)} async-done(((bf16[1536,767]{1,0:T(8,128)(2,1)}), bf16[384,767]{1,0:T(8,128)(2,1)}) %reduce-scatter.26.cloned.1.call-update) | async-done | bytes 589072 | tf_op jit(solution)/shard_map/reduce_scatter | solution.py:261
  703.8 35.6 %reduce-scatter.24.cloned.1.call-done = bf16[192,1536]{1,0:T(8,128)(2,1)} async-done(((bf16[768,1536]{1,0:T(8,128)(2,1)}), bf16[192,1536]{1,0:T(8,128)(2,1)}) %reduce-scatter.24.cloned.1.call-update) | async-done | bytes 589840 | tf_op jit(solution)/shard_map/reduce_scatter | solution.py:255
  739.4 25.2 %reduce-scatter.22.cloned.1.call-done = bf16[96,767]{1,0:T(8,128)(2,1)} async-done(((bf16[384,767]{1,0:T(8,128)(2,1)}), bf16[96,767]{1,0:T(8,128)(2,1)}) %reduce-scatter.22.cloned.1.call-update) | async-done | bytes 147280 | tf_op jit(solution)/shard_map/reduce_scatter | solution.py:252
  764.7 7.0 copy.87
  771.7 9.1 bitcast_convert_fusion
  780.8 3.7 convert_reduce_fusion
  785.8 6.1 all-reduce
  792.0 18.4 %reduce-scatter.16.cloned.1.call-done = bf16[2,512,767]{2,1,0:T(8,128)(2,1)} async-done(((bf16[2,1024,767]{2,1,0:T(8,128)(2,1)}), bf16[2,512,767]{2,1,0:T(8,128)(2,1)}) %reduce-scatter.16.cloned.1.call-update) | async-done | bytes 1570832 | tf_op jit(solution)/shard_map/reduce_scatter | solution.py:164
  813.3 4.9 copy.90
  818.3 14.5 %reduce-scatter.30.cloned.1.call-done = bf16[96,2]{1,0:T(8,128)(2,1)} async-done(((bf16[384,2]{1,0:T(8,128)(2,1)}), bf16[96,2]{1,0:T(8,128)(2,1)}) %reduce-scatter.30.cloned.1.call-update) | async-done | bytes 400
  833.6 11.8 %all-reduce.2 = (bf16[2,96]{1,0:T(2,128)(2,1)S(1)}, bf16[384]{0:T(512)(128)(2,1)S(1)}) all-reduce(bf16[2,96]{1,0:T(2,128)(2,1)S(1)} %copy.97, bf16[384]{0:T(512)(128)(2,1)S(1)} %dynamic-slice.1), channel_id=1, replica_groups=mesh['dp'=4,'group'=4,'tensor'=2] {'group'}, use_global_device_ids=true, to_apply=%region_28.29 | all-reduce | flops 576 | bytes 2304 | tf_op jit(solution)/shard_map/psum | solution.py:267
  846.5 71.2 %all-reduce.6.cloned.1.call-done = (bf16[3,192,384]{1,2,0:T(8,128)(2,1)}, bf16[96,767]{1,0:T(8,128)(2,1)}, bf16[192,1536]{1,0:T(8,128)(2,1)}, bf16[384,767]{1,0:T(8,128)(2,1)}) async-done(((bf16[3,192,384]{1,2,0:T(8,128)(2,1)}, bf16[96,767]{1,0:T(8,128)(2,1)}, bf16[192,1536]{1,0:T(8,128)(2,1)}, bf16[384,767]{1,0:T(8,128)(2,1)}), (bf16[3,192,384]{1,2,0:T(8,128)(2,1)}, bf16[96,767]{1,0:T(8,128)(2,1)}, ...) | async-done | bytes 1768528 | tf_op jit(solution)/shard_map/psum | solution.py:266
  926.1 36.2 %reduce-scatter.20.cloned.1.call-done = bf16[2,512,768]{2,1,0:T(8,128)(2,1)} async-done(((bf16[2,1024,768]{2,1,0:T(8,128)(2,1)}), bf16[2,512,768]{2,1,0:T(8,128)(2,1)}) %reduce-scatter.20.cloned.1.call-update) | async-done | bytes 1572880 | tf_op jit(solution)/shard_map/reduce_scatter | solution.py:222
  974.5 5.2 reshape.591
  979.7 39.6 %all-reduce.1 = (f32[2,768]{1,0:T(2,128)}, f32[2,767]{1,0:T(2,128)}) all-reduce(f32[2,768]{1,0:T(2,128)S(1)} %pad_maximum_fusion.4, f32[2,767]{1,0:T(2,128)S(1)} %pad_maximum_fusion.5), channel_id=1, replica_groups=mesh['dp'=4,'group'=4,'tensor'=2] {'dp','group','tensor'}, use_global_device_ids=true, to_apply=%region_22.23 | all-reduce | flops 3070 | bytes 24560 | tf_op jit(solution)/shard_map/psum | solution.py:236
  (355 shorter events, 203.5 us)
Async XLA Ops:
  7.2 313.1 %copy-start = (bf16[768,1536]{1,0:T(8,128)(2,1)S(1)}, bf16[768,1536]{1,0:T(8,128)(2,1)}, u32[]{:S(2)}) copy-start(bf16[768,1536]{1,0:T(8,128)(2,1)} %param.21) | copy-start | bytes 7077892
  7.2 69.0 %all-gather.5.cloned.1.call-start = ((), (), s32[]{:S(2)}) async-start(), calls=%async_computation.9 | async-start | bytes 4718592 | tf_op jit(solution)/shard_map/all_gather | solution.py:128
  12.4 5.1 copy-start.58
  18.1 6.7 copy-start.40
  18.1 3.9 copy-start.43
  18.3 6.5 copy-start.31
  24.8 3.6 copy-start.51
  24.8 3.5 copy-start.45
  24.9 3.6 copy-start.60
  28.4 199.0 %reduce-scatter.14.cloned.1.call-start = ((), (), s32[]{:S(2)}) async-start(), calls=%async_computation.10 | async-start | bytes 4718592 | tf_op jit(solution)/shard_map/reduce_scatter | solution.py:149
  124.6 54.4 %copy-start.65 = (bf16[384,767]{1,0:T(8,128)(2,1)S(1)}, bf16[384,767]{1,0:T(8,128)(2,1)}, u32[]{:S(2)}) copy-start(bf16[384,767]{1,0:T(8,128)(2,1)} %param.20) | copy-start | bytes 1767172
  131.3 3.7 copy-start.8
  135.0 3.9 copy-start.2
  146.0 4.5 copy-start.36
  158.3 3.7 copy-start.8
  162.0 3.9 copy-start.2
  173.0 4.5 copy-start.36
  183.9 90.0 %all-gather.9.cloned.1.call-start = ((), (), s32[]{:S(2)}) async-start(), calls=%async_computation.13 | async-start | bytes 4712448 | tf_op jit(solution)/shard_map/all_gather | solution.py:172
  184.6 135.7 %all-gather.7.cloned.1.call-start = ((), (), s32[]{:S(2)}) async-start(), calls=%async_computation.11 | async-start | bytes 4718592 | tf_op jit(solution)/shard_map/all_gather | solution.py:155
  231.6 9.2 copy-start.32
  240.8 3.6 copy-start.56
  244.4 155.0 %reduce-scatter.18.cloned.1.call-start = ((), (), s32[]{:S(2)}) async-start(), calls=%async_computation.14 | async-start | bytes 4718592 | tf_op jit(solution)/shard_map/reduce_scatter | solution.py:186
  320.3 13.8 %copy-start.33 = (bf16[96,8,2,1024]{3,1,2,0:T(8,128)(2,1)S(1)}, bf16[96,8,2,1024]{3,1,2,0:T(8,128)(2,1)}, u32[]{:S(2)}) copy-start(bf16[96,8,2,1024]{3,1,2,0:T(8,128)(2,1)} %copy.101) | copy-start | bytes 9437188
  320.3 13.8 %copy-start.63 = (bf16[1536,767]{1,0:T(8,128)(2,1)S(1)}, bf16[1536,767]{1,0:T(8,128)(2,1)}, u32[]{:S(2)}) copy-start(bf16[1536,767]{1,0:T(8,128)(2,1)} %param.23) | copy-start | bytes 7068676
  349.4 6.4 copy-start.68
  355.9 101.4 %all-gather.11.cloned.1.call-start = ((), (), s32[]{:S(2)}) async-start(), calls=%async_computation.15 | async-start | bytes 4712448 | tf_op jit(solution)/shard_map/all_gather | solution.py:194
  359.5 39.9 %copy-start.11 = (f32[2,512,767]{2,1,0:T(8,128)S(1)}, f32[2,512,767]{2,1,0:T(8,128)}, u32[]{:S(2)}) copy-start(f32[2,512,767]{2,1,0:T(8,128)} %get-tuple-element.243) | copy-start | bytes 9424900
  412.3 263.4 %reduce-scatter.28.cloned.1.call-start = ((), (), s32[]{:S(2)}) async-start(), calls=%async_computation.20 | async-start | bytes 2211840
  467.0 5.5 copy-start.3
  476.6 10.7 %copy-start.5 = (pred[512,1024]{1,0:T(8,128)(4,1)}, pred[512,1024]{1,0:T(8,128)(4,1)S(1)}, u32[]{:S(2)}) copy-start(pred[512,1024]{1,0:T(8,128)(4,1)S(1)} %get-tuple-element.421) | copy-start | bytes 1572868 | tf_op jit(solution)/shard_map/while
  510.8 5.2 copy-start.6
  510.8 5.2 copy-start.9
  524.1 7.0 copy-start.4
  543.2 10.7 %copy-start.5 = (pred[512,1024]{1,0:T(8,128)(4,1)}, pred[512,1024]{1,0:T(8,128)(4,1)S(1)}, u32[]{:S(2)}) copy-start(pred[512,1024]{1,0:T(8,128)(4,1)S(1)} %get-tuple-element.421) | copy-start | bytes 1572868 | tf_op jit(solution)/shard_map/while
  577.4 5.2 copy-start.6
  577.4 5.2 copy-start.9
  590.8 7.0 copy-start.4
  606.3 5.6 copy-start.23
  611.9 6.6 copy-start.27
  624.4 3.5 copy-start.61
  638.5 65.3 %reduce-scatter.26.cloned.1.call-start = ((), (), s32[]{:S(2)}) async-start(), calls=%async_computation.19 | async-start | bytes 2949120 | tf_op jit(solution)/shard_map/reduce_scatter | solution.py:261
  638.5 9.4 copy-start.62
  647.9 91.5 %reduce-scatter.24.cloned.1.call-start = ((), (), s32[]{:S(2)}) async-start(), calls=%async_computation.18 | async-start | bytes 2949120 | tf_op jit(solution)/shard_map/reduce_scatter | solution.py:255
  657.4 3.7 copy-start.35
  657.4 107.2 %reduce-scatter.22.cloned.1.call-start = ((), (), s32[]{:S(2)}) async-start(), calls=%async_computation.17 | async-start | bytes 737280 | tf_op jit(solution)/shard_map/reduce_scatter | solution.py:252
  663.4 146.9 %reduce-scatter.16.cloned.1.call-start = ((), (), s32[]{:S(2)}) async-start(), calls=%async_computation.12 | async-start | bytes 4718592 | tf_op jit(solution)/shard_map/reduce_scatter | solution.py:164
  672.5 160.2 %reduce-scatter.30.cloned.1.call-start = ((), (), s32[]{:S(2)}) async-start(), calls=%async_computation.21 | async-start | bytes 122880
  675.7 242.0 %all-reduce.6.cloned.1.call-start = ((), (), s32[]{:S(2)}) async-start(), calls=%async_computation.22 | async-start | bytes 3833856 | tf_op jit(solution)/shard_map/psum | solution.py:266
  764.6 197.6 %reduce-scatter.20.cloned.1.call-start = ((), (), s32[]{:S(2)}) async-start(), calls=%async_computation.16 | async-start | bytes 4718592 | tf_op jit(solution)/shard_map/reduce_scatter | solution.py:222
  764.7 7.1 copy-start.64
  780.8 3.7 copy-start.67
  780.8 5.0 copy-start.57
  780.8 29.5 %copy-start.12 = (f32[2,512,767]{2,1,0:T(8,128)S(1)}, f32[2,512,767]{2,1,0:T(8,128)}, u32[]{:S(2)}) copy-start(f32[2,512,767]{2,1,0:T(8,128)} %get-tuple-element.243) | copy-start | bytes 9424900
  780.8 29.5 %copy-start.55 = (f32[767]{0:T(1024)S(1)}, f32[767]{0:T(1024)}, u32[]{:S(2)}) copy-start(f32[767]{0:T(1024)} %get-tuple-element.192) | copy-start | bytes 9208
  813.3 4.9 copy-start.53
  813.3 4.9 copy-start.54
  818.2 144.0 %copy-start.10 = (f32[2,512,767]{2,1,0:T(8,128)S(1)}, f32[2,512,767]{2,1,0:T(8,128)}, u32[]{:S(2)}) copy-start(f32[2,512,767]{2,1,0:T(8,128)} %convert_element_type.195) | copy-start | bytes 9424900
  818.2 144.0 %copy-start.41 = (f32[768]{0:T(1024)S(1)}, f32[768]{0:T(1024)}, u32[]{:S(2)}) copy-start(f32[768]{0:T(1024)} %copy-done.40) | copy-start | bytes 9220
  818.2 144.0 %copy-start.46 = (f32[2,512]{1,0:T(2,128)S(1)}, f32[2,512]{1,0:T(2,128)}, u32[]{:S(2)}) copy-start(f32[2,512]{1,0:T(2,128)} %copy-done.45) | copy-start | bytes 12292
  923.8 41.2 %copy-start.50 = (f32[1024]{0:T(1024)S(1)}, f32[1024]{0:T(1024)}, u32[]{:S(2)}) copy-start(f32[1024]{0:T(1024)} %copy-done.49) | copy-start | bytes 12292
  964.9 3.3 copy-start.13
  968.3 3.8 copy-start.17
  968.3 3.8 copy-start.48
  972.1 47.2 %copy-start.1 = (bf16[768,1536]{1,0:T(8,128)(2,1)S(1)}, bf16[768,1536]{1,0:T(8,128)(2,1)}, u32[]{:S(2)}) copy-start(bf16[768,1536]{1,0:T(8,128)(2,1)} %param.21) | copy-start | bytes 7077892
  (37 other events, 76.3 us)
Sparse Core Ops, SparseCore 0:
  28.5 47.6 all-gather.4
  184.0 43.3 reduce-scatter.13
  229.0 44.8 all-gather.8
  275.3 44.9 all-gather.6
  356.0 43.3 reduce-scatter.17
  412.4 44.8 all-gather.10
  638.6 29.3 reduce-scatter.27
  670.7 33.0 reduce-scatter.25
  706.3 33.0 reduce-scatter.23
  742.5 22.0 reduce-scatter.21
  766.9 43.3 reduce-scatter.15
  813.2 19.5 reduce-scatter.29
  836.0 81.7 all-reduce.5
  919.8 42.3 reduce-scatter.19
where the time goes:
time: 1040 us; the launch traced here: 1030 us
  waiting for transfers between devices  468 us (45%)
  matrix products  207 us (20%)
  local copies, waits for them, and re-layouts  161 us (15%)
  other arithmetic  114 us (11%)
  blocking collectives  57.5 us (6%)
  between operations  15.8 us (2%)
    psum x1, waiting for transfers between devices, on_device(): lax.psum(shards[0].astype(jnp.bfloat16), 'group').astype(jnp.float32)  71.2 us
    unnamed x134, local copies, waits for them, and re-layouts  50.8 us
    all_gather x1, waiting for transfers between devices, on_device(): full_one = lax.all_gather(one_low, 'tensor', axis=1, tiled=True)  47.5 us
    all_gather x1, waiting for transfers between devices, on_device(): lax.all_gather(branch_seq, 'tensor', axis=1, tiled=True)  44.9 us
    reduce_scatter x1, waiting for transfers between devices, on_device(): lax.psum_scatter(branch_part.astype(jnp.bfloat16), 'tensor', scatter_dime...  42.1 us
    psum x1, blocking collectives, on_device(): lax.psum((gain_terms, bias_terms), ('dp', 'group', 'tensor'))  39.6 us
    all_gather x1, waiting for transfers between devices, on_device(): lax.all_gather(two_low, 'tensor', axis=1, tiled=True)  39.4 us
    reduce_scatter x1, waiting for transfers between devices, on_device(): lax.psum_scatter(two_part.astype(jnp.bfloat16), 'tensor', scatter_dimensi...  37.4 us
  transfers between devices with their start and end apart: 14, of which 13 were waited for; matrix products, arithmetic and copies ran while one was open for 10% of the time, Pallas kernels for 0%

commit v1 on v0

--- a/solution.py
+++ b/solution.py
@@ -263,7 +263,9 @@
         ).astype(jnp.float32),
     )
     reduced = (
-        lax.psum(shards[0].astype(jnp.bfloat16), "group").astype(jnp.float32),
+        jnp.sum(lax.all_gather(shards[0].astype(jnp.bfloat16), "group"), axis=0).astype(
+            jnp.float32
+        ),
         lax.psum(shards[1].astype(jnp.bfloat16), "group").astype(jnp.float32),
         lax.psum(shards[2].astype(jnp.bfloat16), "group").astype(jnp.float32),
         lax.psum(shards[3].astype(jnp.bfloat16), "group").astype(jnp.float32),

time: 1040 us -> 979 us (0.941)
  waiting for transfers between devices: 468 us -> 399 us
    all_gather x0 -> x1, waiting for transfers between devices: none -> 35.8 us  [on_device(): lax.all_gather(shards[0].astype(jnp.bfloat16), 'group')]
    reduce_scatter x1, waiting for transfers between devices: 35.6 us -> 0.02 us  [on_device(): lax.psum_scatter(weight_grads[3].astype(jnp.bfloat16), 'dp', scatter_dime...]
    unnamed x16 -> x17, waiting for transfers between devices: 15.4 us -> 41 us
    reduce_scatter x1, waiting for transfers between devices: 25.3 us -> 0.02 us  [on_device(): lax.psum_scatter(weight_grads[5].astype(jnp.bfloat16), 'dp', scatter_dime...]
    reduce_scatter x1, waiting for transfers between devices: 25.2 us -> 0.02 us  [on_device(): lax.psum_scatter(weight_grads[2].astype(jnp.bfloat16), 'dp', scatter_dime...]
    all_gather x1, waiting for transfers between devices: 44.9 us -> 21.8 us  [on_device(): lax.all_gather(branch_seq, 'tensor', axis=1, tiled=True)]
    psum x1, waiting for transfers between devices: 71.2 us -> 50.2 us  [on_device(): lax.psum(shards[2].astype(jnp.bfloat16), 'group').astype(jnp.float32)]
    unnamed x134 -> x136, local copies, waits for them, and re-layouts: 50.8 us -> 54.4 us
  transfers between devices with their start and end apart: 14 -> 15, of which waited for: 13 -> 12; matrix products, arithmetic and copies ran while one was open for 10% -> 29% of each run, Pallas kernels for 0% -> 0%
where the time goes in v1:
time: 979 us; the launch traced here: 966 us
  waiting for transfers between devices  399 us (41%)
  matrix products  209 us (21%)
  local copies, waits for them, and re-layouts  164 us (17%)
  other arithmetic  117 us (12%)
  blocking collectives  58.5 us (6%)
  between operations  15.5 us (2%)
    unnamed x136, local copies, waits for them, and re-layouts  54.4 us
    psum x1, waiting for transfers between devices, on_device(): lax.psum(shards[2].astype(jnp.bfloat16), 'group').astype(jnp.float32)  50.2 us
    all_gather x1, waiting for transfers between devices, on_device(): full_one = lax.all_gather(one_low, 'tensor', axis=1, tiled=True)  47.5 us
    reduce_scatter x1, waiting for transfers between devices, on_device(): lax.psum_scatter(branch_part.astype(jnp.bfloat16), 'tensor', scatter_dime...  42.1 us
    unnamed x17, waiting for transfers between devices  41 us
    psum x1, blocking collectives, on_device(): lax.psum((gain_terms, bias_terms), ('dp', 'group', 'tensor'))  39.6 us
    all_gather x1, waiting for transfers between devices, on_device(): lax.all_gather(two_low, 'tensor', axis=1, tiled=True)  39.4 us
    reduce_scatter x1, waiting for transfers between devices, on_device(): lax.psum_scatter(one_part.astype(jnp.bfloat16), 'tensor', scatter_dimensi...  37.4 us
  transfers between devices with their start and end apart: 15, of which 12 were waited for; matrix products, arithmetic and copies ran while one was open for 29% of the time, Pallas kernels for 0%

profile of v1, /device:TPU:0, one launch (start us, length us, event | category | flops | bytes accessed | tf_op | source)
XLA Modules:
  0.0 966.5 jit_solution(8114001428074798651)
XLA Ops:
  7.2 5.2 copy.63
  18.4 3.7 copy.65
  28.7 47.5 %all-gather.7.cloned.1.call-done = bf16[2,1024,768]{2,1,0:T(8,128)(2,1)} async-done(((bf16[2,512,768]{2,1,0:T(8,128)(2,1)}), bf16[2,1024,768]{2,1,0:T(8,128)(2,1)}) %all-gather.7.cloned.1.call-update) | async-done | bytes 3145744 | tf_op jit(solution)/shard_map/all_gather | solution.py:128
  76.2 6.8 convolution_bitcast_fusion
  91.0 5.6 squeeze.35
  103.9 3.8 convert_element_type.205
  114.3 5.6 squeeze.34
  124.6 54.3 %while.26 = (s32[]{:T(128)}, bf16[2,1024,6,64]{1,3,2,0:T(8,128)(2,1)}, f32[2,6,1024]{2,1,0:T(8,128)}, bf16[2,1024,6,64]{1,3,2,0:T(8,128)(2,1)}, s32[2,1024]{1,0:...) while((s32[]{:T(128)}, ...), condition=%wide.region_7.8_spmd, body=%wide.region_2.7_spmd.sunk | while | flops 1692272128 | bytes 111457016 | solution.py:144
  127.7 3.6 fusion.157
  131.3 3.6 fusion.158
  135.0 3.9 fusion.159
  146.0 3.9 fusion.162
  154.7 3.6 fusion.157
  158.3 3.6 fusion.158
  162.0 3.9 fusion.159
  172.9 3.9 fusion.162
  178.9 4.9 convolution_convert_fusion.5
  185.3 42.1 %reduce-scatter.14.cloned.1.call-done = bf16[2,512,767]{2,1,0:T(8,128)(2,1)} async-done(((bf16[2,1024,767]{2,1,0:T(8,128)(2,1)}), bf16[2,512,767]{2,1,0:T(8,128)(2,1)}) %reduce-scatter.14.cloned.1.call-update) | async-done | bytes 1570832 | tf_op jit(solution)/shard_map/reduce_scatter | solution.py:149
  227.3 4.1 fusion.94
  235.0 3.9 add_add_fusion.2
  244.4 29.4 %all-gather.11.cloned.1.call-done = bf16[2,1024,767]{1,0,2:T(2,128)(2,1)} async-done(((bf16[2,512,767]{1,0,2:T(2,128)(2,1)}), bf16[2,1024,767]{1,0,2:T(2,128)(2,1)}) %all-gather.11.cloned.1.call-update) | async-done | bytes 3141648 | tf_op jit(solution)/shard_map/all_gather | solution.py:172
  273.9 4.3 pad.21
  280.9 39.4 %all-gather.9.cloned.1.call-done = bf16[2,1024,768]{2,1,0:T(8,128)(2,1)} async-done(((bf16[2,512,768]{2,1,0:T(8,128)(2,1)}), bf16[2,1024,768]{2,1,0:T(8,128)(2,1)}) %all-gather.9.cloned.1.call-update) | async-done | bytes 3145744 | tf_op jit(solution)/shard_map/all_gather | solution.py:155
  320.3 13.9 %multiply_convert_fusion.2 = (bf16[2048,1536]{1,0:T(8,128)(2,1)}, f32[2048,1536]{1,0:T(8,128)}) fusion(f32[1536]{0:T(1024)S(1)} %convert_element_type.210, bf16[2048,768]{1,0:T(8,128)(2,1)} %bitcast.355, bf16[768,1536]{1,0:T(8,128)(2,1)S(1)} %copy-done), kind=kOutput, calls=%fused_computation.125 | convolution fusion | flops 4863295488 | bytes 24385536 | tf_op jit(solution)/shard_map/dot_general | solution.py:156
  334.2 15.3 %fusion.97 = (bf16[1536]{0:T(1024)(128)(2,1)}, bf16[2048,1536]{1,0:T(8,128)(2,1)S(1)}) fusion(f32[2048,1536]{1,0:T(8,128)} %get-tuple-element.272, f32[1536]{0:T(1024)S(1)} %convert_element_type.210, bf16[2048,767]{0,1:T(8,128)(2,1)S(1)} %bitcast.322, bf16[1536,767]{1,0:T(8,128)(2,1)S(1)} %copy-done.64), kind=kOutput, calls=%fused_computation.195 | convolution fusion | flops 4894751232 | bytes 24381440 | tf_op jit(solution)/shard_map/dot_general | solution.py:177
  349.5 6.5 convolution_convert_fusion.2
  362.1 37.4 %reduce-scatter.18.cloned.1.call-done = bf16[2,512,768]{2,1,0:T(8,128)(2,1)} async-done(((bf16[2,1024,768]{2,1,0:T(8,128)(2,1)}), bf16[2,512,768]{2,1,0:T(8,128)(2,1)}) %reduce-scatter.18.cloned.1.call-update) | async-done | bytes 1572880 | tf_op jit(solution)/shard_map/reduce_scatter | solution.py:186
  412.5 9.2 convolution_convert_fusion
  426.3 9.2 convolution_convert_fusion.1
  435.7 21.8 %all-gather.13.cloned.1.call-done = bf16[2,1024,767]{1,0,2:T(2,128)(2,1)} async-done(((bf16[2,512,767]{1,0,2:T(2,128)(2,1)}), bf16[2,1024,767]{1,0,2:T(2,128)(2,1)}) %all-gather.13.cloned.1.call-update) | async-done | bytes 3141648 | tf_op jit(solution)/shard_map/all_gather | solution.py:194
  457.4 4.3 pad.22
  472.7 134.3 %while.27 = (s32[]{:T(128)}, bf16[2,1024,6,64]{1,3,2,0:T(8,128)(2,1)}, bf16[2,1024,6,64]{1,3,2,0:T(8,128)(2,1)}, bf16[2,1024,6,64]{1,3,2,0:T(8,128)(2,1)}, bf16[...) while((s32[]{:T(128)}, ...), condition=%wide.region_17.18_spmd, body=%wide.region_14.17_spmd.sunk | while | flops 4128632320 | bytes 286275584 | solution.py:203
  482.8 4.3 fusion.183
  487.2 5.5 bitcast_dynamic-update-slice_fusion.5
  492.7 8.5 multiply_reduce_fusion.10
  501.1 9.7 %multiply_convert_fusion.7 = bf16[6,512,1024]{2,1,0:T(8,128)(2,1)} fusion(f32[6,512,1024]{2,1,0:T(8,128)} %get-tuple-element.417, f32[6,512,1024]{2,1,0:T(8,128)S(1)} %fusion.175, f32[6,512]{1,0:T(8,128)S(1)} %get-tuple-element.418, f32[6,512]{1,0:T(8,128)S(1)} %get-tuple-element.411, pred[512,1024]{1,0:T(8,128)(4,1)S(1)} %get-tuple-element.416), kind=kLoop, calls=%fused_computation.51.clone.1 | loop fusion | flops 18874368 | bytes 32006144 | tf_op jit(solution)/shard_map/while/body/eval_jaxpr/convert_element_type | solution.py:80
  510.8 5.6 fusion.178
  516.4 8.1 multiply_reduce_fusion.11
  524.5 7.1 multiply_convert_fusion.8
  549.9 4.3 fusion.183
  554.3 5.5 bitcast_dynamic-update-slice_fusion.5
  559.8 8.4 multiply_reduce_fusion.10
  568.3 9.7 %multiply_convert_fusion.7 = bf16[6,512,1024]{2,1,0:T(8,128)(2,1)} fusion(f32[6,512,1024]{2,1,0:T(8,128)} %get-tuple-element.417, f32[6,512,1024]{2,1,0:T(8,128)S(1)} %fusion.175, f32[6,512]{1,0:T(8,128)S(1)} %get-tuple-element.418, f32[6,512]{1,0:T(8,128)S(1)} %get-tuple-element.411, pred[512,1024]{1,0:T(8,128)(4,1)S(1)} %get-tuple-element.416), kind=kLoop, calls=%fused_computation.51.clone.1 | loop fusion | flops 18874368 | bytes 32006144 | tf_op jit(solution)/shard_map/while/body/eval_jaxpr/convert_element_type | solution.py:80
  577.9 5.2 fusion.178
  583.2 8.1 multiply_reduce_fusion.11
  591.3 7.0 multiply_convert_fusion.8
  615.3 3.8 stack.48
  632.9 7.4 convert_bitcast_fusion.1
  640.3 4.0 copy.94
  645.8 9.2 convolution_convert_fusion.3
  659.0 25.0 %reduce-scatter.28.cloned.1.call-done = bf16[192,1152]{1,0:T(8,128)(2,1)} async-done(((bf16[768,1152]{1,0:T(8,128)(2,1)}), bf16[192,1152]{1,0:T(8,128)(2,1)}) %reduce-scatter.28.cloned.1.call-update) | async-done | bytes 442384
  686.3 6.8 copy.85
  693.1 8.2 bitcast_convert_fusion
  701.4 3.7 convert_reduce_fusion
  706.3 6.8 all-reduce
  713.2 16.5 %reduce-scatter.16.cloned.1.call-done = bf16[2,512,767]{2,1,0:T(8,128)(2,1)} async-done(((bf16[2,1024,767]{2,1,0:T(8,128)(2,1)}), bf16[2,512,767]{2,1,0:T(8,128)(2,1)}) %reduce-scatter.16.cloned.1.call-update) | async-done | bytes 1570832 | tf_op jit(solution)/shard_map/reduce_scatter | solution.py:164
  732.7 4.9 copy.90
  737.7 14.5 %reduce-scatter.30.cloned.1.call-done = bf16[96,2]{1,0:T(8,128)(2,1)} async-done(((bf16[384,2]{1,0:T(8,128)(2,1)}), bf16[96,2]{1,0:T(8,128)(2,1)}) %reduce-scatter.30.cloned.1.call-update) | async-done | bytes 400
  752.9 12.1 %all-reduce.2 = (bf16[2,96]{1,0:T(2,128)(2,1)S(1)}, bf16[384]{0:T(512)(128)(2,1)S(1)}) all-reduce(bf16[2,96]{1,0:T(2,128)(2,1)S(1)} %copy.97, bf16[384]{0:T(512)(128)(2,1)S(1)} %dynamic-slice.1), channel_id=1, replica_groups=mesh['dp'=4,'group'=4,'tensor'=2] {'group'}, use_global_device_ids=true, to_apply=%region_28.29 | all-reduce | flops 576 | bytes 2304 | tf_op jit(solution)/shard_map/psum | solution.py:269
  766.2 50.2 %all-reduce.6.cloned.1.call-done = (bf16[96,767]{1,0:T(8,128)(2,1)}, bf16[192,1536]{1,0:T(8,128)(2,1)}, bf16[384,767]{1,0:T(8,128)(2,1)}) async-done(((bf16[96,767]{1,0:T(8,128)(2,1)}, bf16[192,1536]{1,0:T(8,128)(2,1)}, bf16[384,767]{1,0:T(8,128)(2,1)}), (bf16[96,767]{1,0:T(8,128)(2,1)}, bf16[192,1536]{1,0:T(8,128)(2,1)}, bf16[384,767]{1,0:T(8,128)(2,1)})) %all-reduce.6.cloned.1.call-update) | async-done | bytes 1326160 | tf_op jit(solution)/shard_map/psum | solution.py:270
  822.5 35.8 %all-gather.15.cloned.1.call-done = bf16[12,192,384]{2,1,0:T(8,128)(2,1)} async-done(((bf16[3,192,384]{2,1,0:T(8,128)(2,1)}), bf16[12,192,384]{2,1,0:T(8,128)(2,1)}) %all-gather.15.cloned.1.call-update) | async-done | bytes 1769488 | tf_op jit(solution)/shard_map/all_gather | solution.py:266
  865.2 37.4 %reduce-scatter.20.cloned.1.call-done = bf16[2,512,768]{2,1,0:T(8,128)(2,1)} async-done(((bf16[2,1024,768]{2,1,0:T(8,128)(2,1)}), bf16[2,512,768]{2,1,0:T(8,128)(2,1)}) %reduce-scatter.20.cloned.1.call-update) | async-done | bytes 1572880 | tf_op jit(solution)/shard_map/reduce_scatter | solution.py:222
  915.0 5.2 reshape.591
  920.1 39.6 %all-reduce.1 = (f32[2,768]{1,0:T(2,128)}, f32[2,767]{1,0:T(2,128)}) all-reduce(f32[2,768]{1,0:T(2,128)S(1)} %pad_maximum_fusion.4, f32[2,767]{1,0:T(2,128)S(1)} %pad_maximum_fusion.5), channel_id=1, replica_groups=mesh['dp'=4,'group'=4,'tensor'=2] {'dp','group','tensor'}, use_global_device_ids=true, to_apply=%region_22.23 | all-reduce | flops 3070 | bytes 24560 | tf_op jit(solution)/shard_map/psum | solution.py:236
  (362 shorter events, 207.5 us)
Async XLA Ops:
  7.2 313.1 %copy-start = (bf16[768,1536]{1,0:T(8,128)(2,1)S(1)}, bf16[768,1536]{1,0:T(8,128)(2,1)}, u32[]{:S(2)}) copy-start(bf16[768,1536]{1,0:T(8,128)(2,1)} %param.21) | copy-start | bytes 7077892
  7.2 69.0 %all-gather.7.cloned.1.call-start = ((), (), s32[]{:S(2)}) async-start(), calls=%async_computation.9 | async-start | bytes 4718592 | tf_op jit(solution)/shard_map/all_gather | solution.py:128
  12.4 5.0 copy-start.59
  18.1 6.8 copy-start.41
  18.1 4.0 copy-start.44
  18.3 6.6 copy-start.30
  24.9 3.6 copy-start.52
  24.9 3.6 copy-start.46
  24.9 3.6 copy-start.61
  28.5 198.9 %reduce-scatter.14.cloned.1.call-start = ((), (), s32[]{:S(2)}) async-start(), calls=%async_computation.10 | async-start | bytes 4718592 | tf_op jit(solution)/shard_map/reduce_scatter | solution.py:149
  124.6 54.4 %copy-start.66 = (bf16[384,767]{1,0:T(8,128)(2,1)S(1)}, bf16[384,767]{1,0:T(8,128)(2,1)}, u32[]{:S(2)}) copy-start(bf16[384,767]{1,0:T(8,128)(2,1)} %param.20) | copy-start | bytes 1767172
  131.3 3.7 copy-start.8
  135.0 3.9 copy-start.2
  145.9 4.5 copy-start.36
  158.3 3.7 copy-start.8
  162.0 3.9 copy-start.2
  172.9 4.5 copy-start.36
  183.8 90.0 %all-gather.11.cloned.1.call-start = ((), (), s32[]{:S(2)}) async-start(), calls=%async_computation.13 | async-start | bytes 4712448 | tf_op jit(solution)/shard_map/all_gather | solution.py:172
  184.6 135.7 %all-gather.9.cloned.1.call-start = ((), (), s32[]{:S(2)}) async-start(), calls=%async_computation.11 | async-start | bytes 4718592 | tf_op jit(solution)/shard_map/all_gather | solution.py:155
  231.7 9.2 copy-start.31
  240.8 3.6 copy-start.57
  244.4 155.1 %reduce-scatter.18.cloned.1.call-start = ((), (), s32[]{:S(2)}) async-start(), calls=%async_computation.14 | async-start | bytes 4718592 | tf_op jit(solution)/shard_map/reduce_scatter | solution.py:186
  320.3 13.9 %copy-start.34 = (bf16[96,8,2,1024]{3,1,2,0:T(8,128)(2,1)S(1)}, bf16[96,8,2,1024]{3,1,2,0:T(8,128)(2,1)}, u32[]{:S(2)}) copy-start(bf16[96,8,2,1024]{3,1,2,0:T(8,128)(2,1)} %copy.103) | copy-start | bytes 9437188
  320.3 13.9 %copy-start.64 = (bf16[1536,767]{1,0:T(8,128)(2,1)S(1)}, bf16[1536,767]{1,0:T(8,128)(2,1)}, u32[]{:S(2)}) copy-start(bf16[1536,767]{1,0:T(8,128)(2,1)} %param.23) | copy-start | bytes 7068676
  349.5 6.5 copy-start.69
  356.0 101.4 %all-gather.13.cloned.1.call-start = ((), (), s32[]{:S(2)}) async-start(), calls=%async_computation.15 | async-start | bytes 4712448 | tf_op jit(solution)/shard_map/all_gather | solution.py:194
  359.6 39.9 %copy-start.11 = (f32[2,512,767]{2,1,0:T(8,128)S(1)}, f32[2,512,767]{2,1,0:T(8,128)}, u32[]{:S(2)}) copy-start(f32[2,512,767]{2,1,0:T(8,128)} %get-tuple-element.242) | copy-start | bytes 9424900
  412.4 245.8 %reduce-scatter.26.cloned.1.call-start = ((), (), s32[]{:S(2)}) async-start(), calls=%async_computation.19 | async-start | bytes 2949120 | tf_op jit(solution)/shard_map/reduce_scatter | solution.py:261
  421.7 236.5 %reduce-scatter.24.cloned.1.call-start = ((), (), s32[]{:S(2)}) async-start(), calls=%async_computation.18 | async-start | bytes 2949120 | tf_op jit(solution)/shard_map/reduce_scatter | solution.py:255
  435.6 222.7 %reduce-scatter.22.cloned.1.call-start = ((), (), s32[]{:S(2)}) async-start(), calls=%async_computation.17 | async-start | bytes 737280 | tf_op jit(solution)/shard_map/reduce_scatter | solution.py:252
  467.2 5.5 copy-start.3
  476.5 10.7 %copy-start.5 = (pred[512,1024]{1,0:T(8,128)(4,1)}, pred[512,1024]{1,0:T(8,128)(4,1)S(1)}, u32[]{:S(2)}) copy-start(pred[512,1024]{1,0:T(8,128)(4,1)S(1)} %get-tuple-element.420) | copy-start | bytes 1572868 | tf_op jit(solution)/shard_map/while
  510.8 5.6 copy-start.6
  510.8 5.6 copy-start.9
  524.5 7.1 copy-start.4
  543.7 10.6 %copy-start.5 = (pred[512,1024]{1,0:T(8,128)(4,1)}, pred[512,1024]{1,0:T(8,128)(4,1)S(1)}, u32[]{:S(2)}) copy-start(pred[512,1024]{1,0:T(8,128)(4,1)S(1)} %get-tuple-element.420) | copy-start | bytes 1572868 | tf_op jit(solution)/shard_map/while
  577.9 5.2 copy-start.6
  577.9 5.2 copy-start.9
  591.3 7.0 copy-start.4
  607.0 5.6 copy-start.22
  612.6 6.6 copy-start.26
  621.9 4.3 copy-start.35
  629.6 54.3 %reduce-scatter.28.cloned.1.call-start = ((), (), s32[]{:S(2)}) async-start(), calls=%async_computation.21 | async-start | bytes 2211840
  645.7 84.0 %reduce-scatter.16.cloned.1.call-start = ((), (), s32[]{:S(2)}) async-start(), calls=%async_computation.12 | async-start | bytes 4718592 | tf_op jit(solution)/shard_map/reduce_scatter | solution.py:164
  655.0 97.1 %reduce-scatter.30.cloned.1.call-start = ((), (), s32[]{:S(2)}) async-start(), calls=%async_computation.22 | async-start | bytes 122880
  658.2 158.2 %all-reduce.6.cloned.1.call-start = ((), (), s32[]{:S(2)}) async-start(), calls=%async_computation.23 | async-start | bytes 2654208 | tf_op jit(solution)/shard_map/psum | solution.py:270
  658.9 199.4 %all-gather.15.cloned.1.call-start = ((), (), s32[]{:S(2)}) async-start(), calls=%async_computation.20 | async-start | bytes 2211840 | tf_op jit(solution)/shard_map/all_gather | solution.py:266
  686.3 216.4 %reduce-scatter.20.cloned.1.call-start = ((), (), s32[]{:S(2)}) async-start(), calls=%async_computation.16 | async-start | bytes 4718592 | tf_op jit(solution)/shard_map/reduce_scatter | solution.py:222
  686.3 6.8 copy-start.65
  701.3 3.7 copy-start.68
  701.3 5.0 copy-start.58
  701.3 28.3 %copy-start.12 = (f32[2,512,767]{2,1,0:T(8,128)S(1)}, f32[2,512,767]{2,1,0:T(8,128)}, u32[]{:S(2)}) copy-start(f32[2,512,767]{2,1,0:T(8,128)} %get-tuple-element.242) | copy-start | bytes 9424900
  701.4 28.4 %copy-start.56 = (f32[767]{0:T(1024)S(1)}, f32[767]{0:T(1024)}, u32[]{:S(2)}) copy-start(f32[767]{0:T(1024)} %get-tuple-element.192) | copy-start | bytes 9208
  732.7 4.9 copy-start.54
  732.7 4.9 copy-start.55
  820.2 82.5 %copy-start.10 = (f32[2,512,767]{2,1,0:T(8,128)S(1)}, f32[2,512,767]{2,1,0:T(8,128)}, u32[]{:S(2)}) copy-start(f32[2,512,767]{2,1,0:T(8,128)} %convert_element_type.197) | copy-start | bytes 9424900
  820.2 82.5 %copy-start.42 = (f32[768]{0:T(1024)S(1)}, f32[768]{0:T(1024)}, u32[]{:S(2)}) copy-start(f32[768]{0:T(1024)} %copy-done.41) | copy-start | bytes 9220
  820.2 82.5 %copy-start.47 = (f32[2,512]{1,0:T(2,128)S(1)}, f32[2,512]{1,0:T(2,128)}, u32[]{:S(2)}) copy-start(f32[2,512]{1,0:T(2,128)} %copy-done.46) | copy-start | bytes 12292
  863.0 42.4 %copy-start.51 = (f32[1024]{0:T(1024)S(1)}, f32[1024]{0:T(1024)}, u32[]{:S(2)}) copy-start(f32[1024]{0:T(1024)} %copy-done.50) | copy-start | bytes 12292
  905.4 3.3 copy-start.13
  905.4 3.3 copy-start.45
  908.7 3.8 copy-start.17
  908.7 3.8 copy-start.49
  912.5 47.2 %copy-start.1 = (bf16[768,1536]{1,0:T(8,128)(2,1)S(1)}, bf16[768,1536]{1,0:T(8,128)(2,1)}, u32[]{:S(2)}) copy-start(bf16[768,1536]{1,0:T(8,128)(2,1)} %param.21) | copy-start | bytes 7077892
  (39 other events, 80.7 us)
Sparse Core Ops, SparseCore 0:
  28.6 47.6 all-gather.6
  184.0 43.3 reduce-scatter.13
  229.0 44.8 all-gather.10
  275.3 44.9 all-gather.8
  356.1 43.3 reduce-scatter.17
  412.5 44.8 all-gather.12
  460.0 33.0 reduce-scatter.25
  495.8 33.0 reduce-scatter.23
  629.8 22.3 reduce-scatter.21
  654.5 29.3 reduce-scatter.27
  686.3 43.3 reduce-scatter.15
  732.5 19.5 reduce-scatter.29
  754.7 61.5 all-reduce.5
  818.3 39.9 all-gather.14
  860.4 42.2 reduce-scatter.19
